TPU v7x, 32 devices: a whole 2x2x4 slice. The times are simulated.
32 devices in a mesh: freq: 4 (over x, core), space: 8 (over z, y).
Axes of the slice: x: 2, y: 2, z: 4, core: 2. Of those that a mesh axis runs over, the one named last changes fastest.
Arguments:
- source_field: bfloat16 [2, 8, 1024, 1024], P(None, 'freq', 'space'), may hold values from -6 to 6
- receiver_field: bfloat16 [2, 8, 1024, 1024], P(None, 'freq', 'space'), may hold values from -6 to 6
- line_inverse: bfloat16 [2, 8, 1024, 1024], P(None, 'freq'), may hold values from -0.125 to 0.125
- lens_delay: float32 [3, 1024, 1024], P(None, 'space'), may hold values from -0.6 to 0.6
- omegas: float32 [8], P('freq'), may hold values from 4 to 40
- image_weights: float32 [8], P('freq'), may hold values from 0.1 to 1
Outputs:
- source_out: bfloat16 [2, 8, 1024, 1024], P(None, 'freq', 'space')
- receiver_out: bfloat16 [2, 8, 1024, 1024], P(None, 'freq', 'space')
- gradient: float32 [3, 1024, 1024], P(None, 'space')
All inputs are finite; a program needn't handle non-finite values.
Results may differ from a plain program's by a relative error of at most 0.017.
Values may be sent and summed in bfloat16 or wider, within the bound.
No kernel may reach another device: no remote copies, remote signals or barrier semaphores. Data moves between devices by JAX's collectives and lax.ppermute only.
A program may use at most 128 MiB of HBM per device.

v0:
```python
import jax
import jax.numpy as jnp
from jax import lax
from jax.sharding import PartitionSpec as P


def to_blocks(matrix, pieces):
    leading = matrix.shape[:-2]
    local_rows = matrix.shape[-2]
    columns = matrix.shape[-1] // pieces
    arranged = matrix.reshape(leading + (local_rows, pieces, columns))
    arranged = jnp.moveaxis(arranged, -2, -3)
    return arranged.reshape(leading + (pieces, local_rows * columns))


def from_blocks(blocked, local_rows):
    leading = blocked.shape[:-2]
    pieces = blocked.shape[-2]
    columns = blocked.shape[-1] // local_rows
    arranged = blocked.reshape(leading + (pieces, local_rows, columns))
    arranged = jnp.moveaxis(arranged, -1, -3)
    return arranged.reshape(leading + (columns, pieces * local_rows))


def rotate(fields, phase_angle):
    cosine = jnp.cos(phase_angle)
    sine_part = jnp.sin(phase_angle)
    flip_sign = jnp.array([1.0, -1.0], jnp.float32).reshape(2, 1, 1, 1)
    real_part = fields[:, 0]
    imag_part = fields[:, 1]
    return jnp.stack(
        [
            real_part * cosine + flip_sign * imag_part * sine_part,
            imag_part * cosine - flip_sign * real_part * sine_part,
        ],
        axis=1,
    )


def line_solve(line_inverse, fields):
    flip_sign = jnp.array([1.0, -1.0], jnp.float32).reshape(2, 1, 1, 1)
    prod_real = jnp.einsum(
        "fij,wpfrj->wpfri", line_inverse[0], fields, preferred_element_type=jnp.float32
    )
    prod_imag = jnp.einsum(
        "fij,wpfrj->wpfri", line_inverse[1], fields, preferred_element_type=jnp.float32
    )
    new_real = prod_real[:, 0] - flip_sign * prod_imag[:, 1]
    new_imag = prod_real[:, 1] + flip_sign * prod_imag[:, 0]
    return jnp.stack([new_real, new_imag], axis=1)


def march_step(line_inverse, phased, local_rows):
    pieces = lax.axis_size("space")
    across = line_solve(line_inverse, phased).astype(jnp.bfloat16)
    received = lax.all_to_all(
        to_blocks(across, pieces), "space", split_axis=3, concat_axis=3, tiled=True
    )
    return line_solve(line_inverse, from_blocks(received, local_rows))


def image_slice(fields, image_weights):
    image_term = fields[0, 0] * fields[1, 0] + fields[0, 1] * fields[1, 1]
    return jnp.sum(image_weights[:, None, None] * image_term, axis=0)


def reduce_slice(image_term):
    return lax.psum(image_term.astype(jnp.bfloat16), "freq").astype(jnp.float32)


def finish_sums(slices):
    stacked = jnp.stack(slices)
    return stacked


def on_device(source_field, receiver_field, line_inverse, lens_delay, omegas, image_weights):
    pieces = lax.axis_size("space")
    local_rows = lens_delay.shape[1]
    depth_count = lens_delay.shape[0]
    wavefields = jnp.stack([source_field, receiver_field]).astype(jnp.float32)
    slices = []
    lens_columns = from_blocks(
        lax.all_to_all(
            to_blocks(lens_delay, pieces), "space", split_axis=1, concat_axis=1, tiled=True
        ),
        local_rows,
    )
    phased = rotate(wavefields, omegas[:, None, None] * lens_delay[0][None]).astype(jnp.bfloat16)
    solved = march_step(line_inverse, phased, local_rows)
    slices.append(reduce_slice(image_slice(solved, image_weights)))
    for depth_step in range(1, depth_count):
        phase_angle = omegas[:, None, None] * lens_columns[depth_step][None]
        phased_columns = rotate(solved, phase_angle).astype(jnp.bfloat16)
        received = lax.all_to_all(
            to_blocks(phased_columns, pieces), "space", split_axis=3, concat_axis=3, tiled=True
        )
        solved = march_step(line_inverse, from_blocks(received, local_rows), local_rows)
        slices.append(reduce_slice(image_slice(solved, image_weights)))
    final_blocks = lax.all_to_all(
        to_blocks(solved.astype(jnp.bfloat16), pieces),
        "space",
        split_axis=3,
        concat_axis=3,
        tiled=True,
    )
    final_fields = from_blocks(final_blocks, local_rows)
    gradient_columns = finish_sums(slices)
    gradient = from_blocks(
        lax.all_to_all(
            to_blocks(gradient_columns, pieces).astype(jnp.bfloat16),
            "space",
            split_axis=1,
            concat_axis=1,
            tiled=True,
        ).astype(jnp.float32),
        local_rows,
    )
    return (final_fields[0], final_fields[1], gradient)


def solution(mesh):
    placed = (
        P(None, "freq", "space", None),
        P(None, "freq", "space", None),
        P(None, "freq", None, None),
        P(None, "space", None),
        P("freq"),
        P("freq"),
    )
    return jax.shard_map(
        on_device,
        mesh=mesh,
        in_specs=placed,
        out_specs=(
            P(None, "freq", "space", None),
            P(None, "freq", "space", None),
            P(None, "space", None),
        ),
        check_vma=False,
    )
```

profile of v0, /device:TPU:0, one launch (start us, length us, event | category | flops | bytes accessed | tf_op | source)
XLA Modules:
  0.0 648.7 jit_solution(17331599846674338511)
XLA Ops:
  9.1 2.5 copy.277
  11.5 7.4 %all-to-all-start.1 = ((f32[3,8,16384]{2,0,1:T(4,128)}), f32[3,8,16384]{2,0,1:T(4,128)S(1)}, u32[]{:S(2)}, u32[]{:S(2)}) async-start(f32[3,8,16384]{2,0,1:T(4,128)} %copy.277), calls=%async_computation.1 | async-start | bytes 4194304 | tf_op jit(solution)/shard_map/all_to_all | solution.py:83
  24.5 42.7 %all-to-all-done.1 = f32[3,8,16384]{2,0,1:T(4,128)S(1)} async-done(((f32[3,8,16384]{2,0,1:T(4,128)}), f32[3,8,16384]{2,0,1:T(4,128)S(1)}, u32[]{:S(2)}, u32[]{:S(2)}) %all-to-all-start.1) | async-done | bytes 1572896 | tf_op jit(solution)/shard_map/all_to_all | solution.py:83
  71.8 12.3 %multiply_cosine_fusion.2 = (f32[2,128,1024]{2,1,0:T(8,128)S(1)}, f32[2,128,1024]{2,1,0:T(8,128)S(1)}, f32[2,128,1024]{2,1,0:T(8,128)}, f32[2,128,1024]{2,1,0:T(...) fusion(f32[128,1024]{1,0:T(8,128)S(1)} %copy-done.20, f32[2]{0:T(128)S(1)} %copy-done.28, ...), kind=kLoop, calls=%fused_computation.110 | loop fusion | flops 786432 | bytes 7864328 | tf_op jit(solution)/shard_map/cos | solution.py:26
  85.2 4.7 fusion.33
  90.0 2.4 fusion.51
  94.9 2.8 reshape.190
  97.7 3.7 copy.270
  101.4 51.8 %all_to_all.40 = bf16[2,2,2,8,16384]{4,2,1,0,3:T(2,128)(2,1)S(1)} all-to-all(bf16[2,2,2,8,16384]{4,2,1,0,3:T(2,128)(2,1)S(1)} %copy.270), channel_id=1, replica_groups=mesh['freq'=4,'space'=8] {'space'}, dimensions={3} | all-to-all | bytes 4194304 | tf_op jit(solution)/shard_map/all_to_all | solution.py:56
  153.3 2.8 reshape.220
  156.1 3.1 copy.343
  161.5 5.3 fusion.27
  166.9 6.1 fusion.45
  178.9 3.7 copy.285
  182.7 51.6 %all_to_all.41 = bf16[2,2,2,8,16384]{4,2,1,0,3:T(2,128)(2,1)S(1)} all-to-all(bf16[2,2,2,8,16384]{4,2,1,0,3:T(2,128)(2,1)S(1)} %copy.285), channel_id=1, replica_groups=mesh['freq'=4,'space'=8] {'space'}, dimensions={3} | all-to-all | bytes 4194304 | tf_op jit(solution)/shard_map/all_to_all | solution.py:94
  234.2 2.8 reshape.223
  237.1 3.1 copy.287
  242.5 5.3 fusion.36
  247.8 4.6 fusion.54
  257.2 3.7 copy.290
  261.0 51.4 %all_to_all.42 = bf16[2,2,2,8,16384]{4,2,1,0,3:T(2,128)(2,1)S(1)} all-to-all(bf16[2,2,2,8,16384]{4,2,1,0,3:T(2,128)(2,1)S(1)} %copy.290), channel_id=1, replica_groups=mesh['freq'=4,'space'=8] {'space'}, dimensions={3} | all-to-all | bytes 4194304 | tf_op jit(solution)/shard_map/all_to_all | solution.py:56
  312.4 2.8 reshape.224
  315.2 3.1 copy.350
  320.6 5.3 fusion.30
  326.0 6.1 fusion.48
  335.6 2.3 reshape.202
  338.0 3.7 copy.302
  341.7 51.6 %all_to_all.43 = bf16[2,2,2,8,16384]{4,2,1,0,3:T(2,128)(2,1)S(1)} all-to-all(bf16[2,2,2,8,16384]{4,2,1,0,3:T(2,128)(2,1)S(1)} %copy.302), channel_id=1, replica_groups=mesh['freq'=4,'space'=8] {'space'}, dimensions={3} | all-to-all | bytes 4194304 | tf_op jit(solution)/shard_map/all_to_all | solution.py:94
  393.3 2.8 reshape.226
  396.1 3.1 copy.304
  401.6 5.3 fusion.39
  406.9 4.6 fusion.57
  416.3 3.7 copy.307
  420.1 51.4 %all_to_all.44 = bf16[2,2,2,8,16384]{4,2,1,0,3:T(2,128)(2,1)S(1)} all-to-all(bf16[2,2,2,8,16384]{4,2,1,0,3:T(2,128)(2,1)S(1)} %copy.307), channel_id=1, replica_groups=mesh['freq'=4,'space'=8] {'space'}, dimensions={3} | all-to-all | bytes 4194304 | tf_op jit(solution)/shard_map/all_to_all | solution.py:56
  471.5 2.8 reshape.227
  474.3 3.1 copy.356
  479.7 5.3 fusion.24
  485.1 8.1 %fusion.42 = f32[2,2,2,128,1024]{4,3,2,0,1:T(8,128)} fusion(bf16[2,2,2,128,1024]{4,3,2,0,1:T(8,128)(2,1)S(1)} %copy-done.25, bf16[2,2,1024,1024]{3,2,1,0:T(8,128)(2,1)} %param.17), kind=kOutput, calls=%fused_computation.30 | convolution fusion | flops 2147483648 | bytes 10485760 | tf_op jit(solution)/shard_map/fij,wpfrj->wpfri/dot_general | solution.py:42
  493.2 6.4 fusion.72
  499.7 6.2 subtract_convert_fusion
  512.9 34.0 %all-reduce.3.cloned.1.call-done = (bf16[1,128,8,128]{1,3,2,0:T(8,128)(2,1)}, bf16[1,128,8,128]{1,3,2,0:T(8,128)(2,1)}, bf16[1,128,8,128]{1,3,2,0:T(8,128)(2,1)}) async-done(((bf16[1,128,8,128]{1,3,2,0:T(8,128)(2,1)}, bf16[1,128,8,128]{1,3,2,0:T(8,128)(2,1)}, bf16[1,128,8,128]{1,3,2,0:T(8,128)(2,1)}), (bf16[1,128,8,128]{1,3,2,0:T(8,128)(2,1)}, bf16[1,128,8,128]{1,3,2,0:T(8,128)(2,1)}, ...) | async-done | bytes 786448 | tf_op jit(solution)/shard_map/psum | solution.py:68
  551.6 5.8 all-to-all-start.7
  562.9 5.1 copy.317
  568.0 14.5 %all-to-all-done.7 = bf16[3,8,16384]{2,0,1:T(4,128)(2,1)S(1)} async-done(((bf16[3,8,16384]{2,0,1:T(4,128)(2,1)}), bf16[3,8,16384]{2,0,1:T(4,128)(2,1)S(1)}, u32[]{:S(2)}, u32[]{:S(2)}) %all-to-all-start.7) | async-done | bytes 786464 | tf_op jit(solution)/shard_map/all_to_all | solution.py:109
  582.5 3.6 all-to-all-start.6
  588.2 3.0 copy.329
  591.2 43.1 %all-to-all-done.6 = bf16[2,2,2,8,16384]{4,2,1,0,3:T(2,128)(2,1)S(1)} async-done(((bf16[2,2,2,8,16384]{4,2,1,0,3:T(2,128)(2,1)}), bf16[2,2,2,8,16384]{4,2,1,0,3:T(2,128)(2,1)S(1)}, u32[]{:S(2)}, u32[]{:S(2)}) %all-to-all-start.6) | async-done | bytes 2097184 | tf_op jit(solution)/shard_map/all_to_all | solution.py:99
  634.3 2.8 reshape.229
  (137 shorter events, 69.8 us)
Async XLA Ops:
  11.5 7.5 %copy-start.26 = (bf16[2,2,128,1024]{3,2,1,0:T(8,128)(2,1)S(1)}, bf16[2,2,128,1024]{3,2,1,0:T(8,128)(2,1)}, u32[]{:S(2)}) copy-start(bf16[2,2,128,1024]{3,2,1,0:T(8,128)(2,1)} %param.16) | copy-start | bytes 3145732
  11.5 55.7 %all-to-all-start.1 = ((f32[3,8,16384]{2,0,1:T(4,128)}), f32[3,8,16384]{2,0,1:T(4,128)S(1)}, u32[]{:S(2)}, u32[]{:S(2)}) async-start(f32[3,8,16384]{2,0,1:T(4,128)} %copy.277), calls=%async_computation.1 | async-start | bytes 4194304 | tf_op jit(solution)/shard_map/all_to_all | solution.py:83
  18.9 528.0 %all-reduce.3.cloned.1.call-start = ((), (), s32[]{:S(2)}) async-start(), calls=%async_computation.8 | async-start | bytes 1572864 | tf_op jit(solution)/shard_map/psum | solution.py:68
  70.8 1.0 copy-start.20
  70.8 1.0 copy-start.28
  71.8 12.3 %copy-start.8 = (f32[2,2,2,128,1024]{4,3,1,0,2:T(8,128)S(1)}, f32[2,2,2,128,1024]{4,3,1,0,2:T(8,128)}, u32[]{:S(2)}) copy-start(f32[2,2,2,128,1024]{4,3,1,0,2:T(8,128)} %maximum_convert_fusion) | copy-start | bytes 12582916
  71.8 12.3 %copy-start.27 = (f32[2]{0:T(128)S(1)}, f32[2]{0:T(128)}, u32[]{:S(2)}) copy-start(f32[2]{0:T(128)} %constant.4.clone) | copy-start | bytes 28
  84.2 5.8 slice-start
  85.2 4.8 slice-start.1
  161.5 5.3 copy-start.21
  166.8 6.2 copy-start
  166.9 6.2 copy-start.18
  166.9 6.2 copy-start.19
  173.0 2.3 copy-start.2
  242.5 5.3 copy-start.22
  320.6 5.3 copy-start.23
  326.0 6.1 copy-start.4
  326.0 6.1 copy-start.17
  332.1 2.3 copy-start.6
  401.6 5.3 copy-start.24
  479.7 5.3 copy-start.25
  479.7 13.5 %copy-start.7 = (f32[2,2,2,128,1024]{4,3,2,0,1:T(8,128)S(1)}, f32[2,2,2,128,1024]{4,3,2,0,1:T(8,128)}, u32[]{:S(2)}) copy-start(f32[2,2,2,128,1024]{4,3,2,0,1:T(8,128)} %copy-done.6) | copy-start | bytes 12582916
  485.1 8.2 %copy-start.9 = (f32[2,2,2,128,1024]{4,3,2,0,1:T(8,128)}, f32[2,2,2,128,1024]{4,3,2,0,1:T(8,128)S(1)}, u32[]{:S(2)}) copy-start(f32[2,2,2,128,1024]{4,3,2,0,1:T(8,128)S(1)} %fusion.24) | copy-start | bytes 12582916
  485.1 8.2 %copy-start.1 = (f32[2,2,2,128,1024]{4,3,2,0,1:T(8,128)S(1)}, f32[2,2,2,128,1024]{4,3,2,0,1:T(8,128)}, u32[]{:S(2)}) copy-start(f32[2,2,2,128,1024]{4,3,2,0,1:T(8,128)} %copy-done) | copy-start | bytes 12582916
  485.1 8.2 %copy-start.3 = (f32[2,2,2,128,1024]{4,3,2,0,1:T(8,128)S(1)}, f32[2,2,2,128,1024]{4,3,2,0,1:T(8,128)}, u32[]{:S(2)}) copy-start(f32[2,2,2,128,1024]{4,3,2,0,1:T(8,128)} %copy-done.2) | copy-start | bytes 12582916
  485.1 8.2 %copy-start.5 = (f32[2,2,2,128,1024]{4,3,2,0,1:T(8,128)S(1)}, f32[2,2,2,128,1024]{4,3,2,0,1:T(8,128)}, u32[]{:S(2)}) copy-start(f32[2,2,2,128,1024]{4,3,2,0,1:T(8,128)} %copy-done.4) | copy-start | bytes 12582916
  499.6 6.2 copy-start.10
  499.6 6.7 %copy-start.14 = (f32[2,2,128,1024]{3,2,1,0:T(8,128)S(1)}, f32[2,2,128,1024]{3,2,1,0:T(8,128)}, u32[]{:S(2)}) copy-start(f32[2,2,128,1024]{3,2,1,0:T(8,128)} %get-tuple-element.57) | copy-start | bytes 6291460
  499.7 6.7 %copy-start.15 = (f32[2,2,128,1024]{3,2,1,0:T(8,128)S(1)}, f32[2,2,128,1024]{3,2,1,0:T(8,128)}, u32[]{:S(2)}) copy-start(f32[2,2,128,1024]{3,2,1,0:T(8,128)} %get-tuple-element.58) | copy-start | bytes 6291460
  505.9 1.6 copy-start.11
  505.9 2.2 copy-start.12
  505.9 2.9 copy-start.13
  505.9 2.8 copy-start.29
  551.6 30.8 %all-to-all-start.7 = ((bf16[3,8,16384]{2,0,1:T(4,128)(2,1)}), bf16[3,8,16384]{2,0,1:T(4,128)(2,1)S(1)}, u32[]{:S(2)}, u32[]{:S(2)}) async-start(bf16[3,8,16384]{2,0,1:T(4,128)(2,1)} %reshape.230), calls=%async_computation.7 | async-start | bytes 2097152 | tf_op jit(solution)/shard_map/all_to_all | solution.py:109
  557.4 1.9 copy-start.16
  582.5 51.8 %all-to-all-start.6 = ((bf16[2,2,2,8,16384]{4,2,1,0,3:T(2,128)(2,1)}), bf16[2,2,2,8,16384]{4,2,1,0,3:T(2,128)(2,1)S(1)}, u32[]{:S(2)}, u32[]{:S(2)}) async-start(bf16[2,2,2,8,16384]{4,2,1,0,3:T(2,128)(2,1)} %copy.317), calls=%async_computation.6 | async-start | bytes 4194304 | tf_op jit(solution)/shard_map/all_to_all | solution.py:99
Sparse Core Ops, SparseCore 0:
  513.0 33.8 all-reduce.2
where the time goes:
time: 659 us; the launch traced here: 649 us
  blocking collectives  258 us (39%)
  waiting for transfers between devices  134 us (20%)
  local copies, waits for them, and re-layouts  120 us (18%)
  matrix products  63.2 us (10%)
  other arithmetic  41.5 us (6%)
  starting transfers between devices  16.8 us (3%)
  between operations  15.1 us (2%)
    all_to_all x3, blocking collectives, march_step(): lax.all_to_all(to_blocks(across, pieces), 'space', split_axis=3, concat_a...  155 us
    all_to_all x2, blocking collectives, on_device(): lax.all_to_all(to_blocks(phased_columns, pieces), 'space', split_axis=3,...  103 us
    all_to_all x1, waiting for transfers between devices, on_device(): lax.all_to_all(to_blocks(solved.astype(jnp.bfloat16), pieces), 'space', s...  43.1 us
    all_to_all x1, waiting for transfers between devices, on_device(): lax.all_to_all(to_blocks(lens_delay, pieces), 'space', split_axis=1, conc...  42.7 us
    reshape x14, local copies, waits for them, and re-layouts, to_blocks(): return arranged.reshape(leading + (pieces, local_rows * columns))  41 us
    psum x1, waiting for transfers between devices, reduce_slice(): return lax.psum(image_term.astype(jnp.bfloat16), 'freq').astype(jnp.float32)  34 us
    dot_general x6, matrix products, line_solve(): jnp.einsum('fij,wpfrj->wpfri', line_inverse[0], fields, preferred_element...  31.8 us
    dot_general x6, matrix products, line_solve(): jnp.einsum('fij,wpfrj->wpfri', line_inverse[1], fields, preferred_element...  31.4 us
  transfers between devices with their start and end apart: 4, of which 4 were waited for; matrix products, arithmetic and copies ran while one was open for 3% of the time, Pallas kernels for 0%

commit v1 on v0

--- a/solution.py
+++ b/solution.py
@@ -2,6 +2,12 @@
 import jax.numpy as jnp
 from jax import lax
 from jax.sharding import PartitionSpec as P
+
+
+def summed_here(array, name):
+    parts = lax.all_gather(array, name, axis=0, tiled=False)
+    acc = parts.sum(axis=0)
+    return acc
 
 
 def to_blocks(matrix, pieces):
@@ -65,7 +71,7 @@
 
 
 def reduce_slice(image_term):
-    return lax.psum(image_term.astype(jnp.bfloat16), "freq").astype(jnp.float32)
+    return summed_here(image_term.astype(jnp.bfloat16), "freq").astype(jnp.float32)
 
 
 def finish_sums(slices):

time: 659 us -> 678 us (1.029)
  waiting for transfers between devices: 134 us -> 151 us
    all_gather x0 -> x3, waiting for transfers between devices: none -> 48.2 us  [summed_here(): parts = lax.all_gather(array, name, axis=0, tiled=False)]
    psum x1 -> x0, waiting for transfers between devices: 34 us -> none  [reduce_slice(): return lax.psum(image_term.astype(jnp.bfloat16), 'freq').astype(jnp.float32)]
  transfers between devices with their start and end apart: 4 -> 6, of which waited for: 4 -> 6; matrix products, arithmetic and copies ran while one was open for 3% -> 4% of each run, Pallas kernels for 0% -> 0%
where the time goes in v1:
time: 678 us; the launch traced here: 667 us
  blocking collectives  258 us (38%)
  waiting for transfers between devices  151 us (22%)
  local copies, waits for them, and re-layouts  118 us (17%)
  matrix products  63.2 us (9%)
  other arithmetic  45.7 us (7%)
  starting transfers between devices  17 us (3%)
  between operations  14.8 us (2%)
    all_to_all x3, blocking collectives, march_step(): lax.all_to_all(to_blocks(across, pieces), 'space', split_axis=3, concat_a...  155 us
    all_to_all x2, blocking collectives, on_device(): lax.all_to_all(to_blocks(phased_columns, pieces), 'space', split_axis=3,...  103 us
    all_gather x3, waiting for transfers between devices, summed_here(): parts = lax.all_gather(array, name, axis=0, tiled=False)  48.2 us
    all_to_all x1, waiting for transfers between devices, on_device(): lax.all_to_all(to_blocks(solved.astype(jnp.bfloat16), pieces), 'space', s...  43.4 us
    all_to_all x1, waiting for transfers between devices, on_device(): lax.all_to_all(to_blocks(lens_delay, pieces), 'space', split_axis=1, conc...  42.7 us
    reshape x14, local copies, waits for them, and re-layouts, to_blocks(): return arranged.reshape(leading + (pieces, local_rows * columns))  41 us
    dot_general x6, matrix products, line_solve(): jnp.einsum('fij,wpfrj->wpfri', line_inverse[0], fields, preferred_element...  31.8 us
    dot_general x6, matrix products, line_solve(): jnp.einsum('fij,wpfrj->wpfri', line_inverse[1], fields, preferred_element...  31.4 us
  transfers between devices with their start and end apart: 6, of which 6 were waited for; matrix products, arithmetic and copies ran while one was open for 4% of the time, Pallas kernels for 0%

profile of v1, /device:TPU:0, one launch (start us, length us, event | category | flops | bytes accessed | tf_op | source)
XLA Modules:
  0.0 667.5 jit_solution(9960343961219125715)
XLA Ops:
  11.5 7.4 %all-to-all-start.1 = ((f32[3,8,16384]{2,0,1:T(4,128)}), f32[3,8,16384]{2,0,1:T(4,128)S(1)}, u32[]{:S(2)}, u32[]{:S(2)}) async-start(f32[3,8,16384]{2,0,1:T(4,128)} %copy.277), calls=%async_computation.1 | async-start | bytes 4194304 | tf_op jit(solution)/shard_map/all_to_all | solution.py:89
  24.5 42.7 %all-to-all-done.1 = f32[3,8,16384]{2,0,1:T(4,128)S(1)} async-done(((f32[3,8,16384]{2,0,1:T(4,128)}), f32[3,8,16384]{2,0,1:T(4,128)S(1)}, u32[]{:S(2)}, u32[]{:S(2)}) %all-to-all-start.1) | async-done | bytes 1572896 | tf_op jit(solution)/shard_map/all_to_all | solution.py:89
  71.8 12.3 %multiply_cosine_fusion.2 = (f32[2,128,1024]{2,1,0:T(8,128)S(1)}, f32[2,128,1024]{2,1,0:T(8,128)S(1)}, f32[2,128,1024]{2,1,0:T(8,128)}, f32[2,128,1024]{2,1,0:T(...) fusion(f32[128,1024]{1,0:T(8,128)S(1)} %copy-done.20, f32[2]{0:T(128)S(1)} %copy-done.28, ...), kind=kLoop, calls=%fused_computation.110 | loop fusion | flops 786432 | bytes 7864328 | tf_op jit(solution)/shard_map/cos | solution.py:32
  85.3 4.7 fusion.33
  94.9 2.8 reshape.247
  97.7 3.7 copy.270
  101.5 51.8 %all_to_all.40 = bf16[2,2,2,8,16384]{4,2,1,0,3:T(2,128)(2,1)S(1)} all-to-all(bf16[2,2,2,8,16384]{4,2,1,0,3:T(2,128)(2,1)S(1)} %copy.270), channel_id=1, replica_groups=mesh['freq'=4,'space'=8] {'space'}, dimensions={3} | all-to-all | bytes 4194304 | tf_op jit(solution)/shard_map/all_to_all | solution.py:62
  153.3 2.8 reshape.280
  156.1 3.1 copy.343
  161.5 5.3 fusion.27
  166.9 6.1 fusion.45
  178.9 3.7 copy.285
  182.7 51.6 %all_to_all.41 = bf16[2,2,2,8,16384]{4,2,1,0,3:T(2,128)(2,1)S(1)} all-to-all(bf16[2,2,2,8,16384]{4,2,1,0,3:T(2,128)(2,1)S(1)} %copy.285), channel_id=1, replica_groups=mesh['freq'=4,'space'=8] {'space'}, dimensions={3} | all-to-all | bytes 4194304 | tf_op jit(solution)/shard_map/all_to_all | solution.py:100
  234.3 2.8 reshape.283
  237.1 3.1 copy.287
  242.5 5.3 fusion.36
  247.8 4.6 fusion.54
  257.3 3.7 copy.290
  261.0 51.4 %all_to_all.42 = bf16[2,2,2,8,16384]{4,2,1,0,3:T(2,128)(2,1)S(1)} all-to-all(bf16[2,2,2,8,16384]{4,2,1,0,3:T(2,128)(2,1)S(1)} %copy.290), channel_id=1, replica_groups=mesh['freq'=4,'space'=8] {'space'}, dimensions={3} | all-to-all | bytes 4194304 | tf_op jit(solution)/shard_map/all_to_all | solution.py:62
  312.4 2.8 reshape.284
  315.2 3.1 copy.350
  320.7 5.3 fusion.30
  326.0 6.1 fusion.48
  338.0 3.7 copy.302
  341.7 51.6 %all_to_all.43 = bf16[2,2,2,8,16384]{4,2,1,0,3:T(2,128)(2,1)S(1)} all-to-all(bf16[2,2,2,8,16384]{4,2,1,0,3:T(2,128)(2,1)S(1)} %copy.302), channel_id=1, replica_groups=mesh['freq'=4,'space'=8] {'space'}, dimensions={3} | all-to-all | bytes 4194304 | tf_op jit(solution)/shard_map/all_to_all | solution.py:100
  393.3 2.8 reshape.286
  396.1 3.1 copy.304
  401.6 5.3 fusion.39
  406.9 4.6 fusion.57
  416.3 3.7 copy.307
  420.1 51.4 %all_to_all.44 = bf16[2,2,2,8,16384]{4,2,1,0,3:T(2,128)(2,1)S(1)} all-to-all(bf16[2,2,2,8,16384]{4,2,1,0,3:T(2,128)(2,1)S(1)} %copy.307), channel_id=1, replica_groups=mesh['freq'=4,'space'=8] {'space'}, dimensions={3} | all-to-all | bytes 4194304 | tf_op jit(solution)/shard_map/all_to_all | solution.py:62
  471.4 2.8 reshape.287
  474.2 3.1 copy.356
  479.6 5.3 fusion.24
  485.0 8.1 %fusion.42 = f32[2,2,2,128,1024]{4,3,2,0,1:T(8,128)} fusion(bf16[2,2,2,128,1024]{4,3,2,0,1:T(8,128)(2,1)S(1)} %copy-done.25, bf16[2,2,1024,1024]{3,2,1,0:T(8,128)(2,1)} %param.17), kind=kOutput, calls=%fused_computation.30 | convolution fusion | flops 2147483648 | bytes 10485760 | tf_op jit(solution)/shard_map/fij,wpfrj->wpfri/dot_general | solution.py:48
  493.2 6.4 fusion.72
  499.7 6.2 subtract_convert_fusion
  508.7 2.6 fusion.103
  512.8 14.3 %all-gather.7.cloned.1.call-done = bf16[512,1024]{1,0:T(8,128)(2,1)} async-done(((bf16[128,1024]{1,0:T(8,128)(2,1)}), bf16[512,1024]{1,0:T(8,128)(2,1)}) %all-gather.7.cloned.1.call-update) | async-done | bytes 1048592 | tf_op jit(solution)/shard_map/all_gather | solution.py:8
  528.7 17.3 %all-gather.9.cloned.1.call-done = bf16[512,1024]{1,0:T(8,128)(2,1)} async-done(((bf16[128,1024]{1,0:T(8,128)(2,1)}), bf16[512,1024]{1,0:T(8,128)(2,1)}) %all-gather.9.cloned.1.call-update) | async-done | bytes 1048592 | tf_op jit(solution)/shard_map/all_gather | solution.py:8
  547.6 16.7 %all-gather.11.cloned.1.call-done = bf16[512,1024]{1,0:T(8,128)(2,1)} async-done(((bf16[128,1024]{1,0:T(8,128)(2,1)}), bf16[512,1024]{1,0:T(8,128)(2,1)}) %all-gather.11.cloned.1.call-update) | async-done | bytes 1048592 | tf_op jit(solution)/shard_map/all_gather | solution.py:8
  569.5 5.8 all-to-all-start.7
  580.8 5.1 copy.317
  585.9 15.5 %all-to-all-done.7 = bf16[3,8,16384]{2,0,1:T(4,128)(2,1)S(1)} async-done(((bf16[3,8,16384]{2,0,1:T(4,128)(2,1)}), bf16[3,8,16384]{2,0,1:T(4,128)(2,1)S(1)}, u32[]{:S(2)}, u32[]{:S(2)}) %all-to-all-start.7) | async-done | bytes 786464 | tf_op jit(solution)/shard_map/all_to_all | solution.py:115
  601.4 3.6 all-to-all-start.6
  607.0 3.0 copy.329
  610.1 43.4 %all-to-all-done.6 = bf16[2,2,2,8,16384]{4,2,1,0,3:T(2,128)(2,1)S(1)} async-done(((bf16[2,2,2,8,16384]{4,2,1,0,3:T(2,128)(2,1)}), bf16[2,2,2,8,16384]{4,2,1,0,3:T(2,128)(2,1)S(1)}, u32[]{:S(2)}, u32[]{:S(2)}) %all-to-all-start.6) | async-done | bytes 2097184 | tf_op jit(solution)/shard_map/all_to_all | solution.py:105
  653.4 2.8 reshape.289
  (146 shorter events, 78.0 us)
Async XLA Ops:
  11.5 7.5 %copy-start.26 = (bf16[2,2,128,1024]{3,2,1,0:T(8,128)(2,1)S(1)}, bf16[2,2,128,1024]{3,2,1,0:T(8,128)(2,1)}, u32[]{:S(2)}) copy-start(bf16[2,2,128,1024]{3,2,1,0:T(8,128)(2,1)} %param.16) | copy-start | bytes 3145732
  11.5 55.7 %all-to-all-start.1 = ((f32[3,8,16384]{2,0,1:T(4,128)}), f32[3,8,16384]{2,0,1:T(4,128)S(1)}, u32[]{:S(2)}, u32[]{:S(2)}) async-start(f32[3,8,16384]{2,0,1:T(4,128)} %copy.277), calls=%async_computation.1 | async-start | bytes 4194304 | tf_op jit(solution)/shard_map/all_to_all | solution.py:89
  19.0 508.2 %all-gather.7.cloned.1.call-start = ((), (), s32[]{:S(2)}) async-start(), calls=%async_computation.8 | async-start | bytes 1310720 | tf_op jit(solution)/shard_map/all_gather | solution.py:8
  70.8 1.0 copy-start.20
  70.8 1.0 copy-start.28
  71.8 12.3 %copy-start.8 = (f32[2,2,2,128,1024]{4,3,1,0,2:T(8,128)S(1)}, f32[2,2,2,128,1024]{4,3,1,0,2:T(8,128)}, u32[]{:S(2)}) copy-start(f32[2,2,2,128,1024]{4,3,1,0,2:T(8,128)} %maximum_convert_fusion) | copy-start | bytes 12582916
  71.8 12.3 %copy-start.27 = (f32[2]{0:T(128)S(1)}, f32[2]{0:T(128)}, u32[]{:S(2)}) copy-start(f32[2]{0:T(128)} %constant.8.clone) | copy-start | bytes 28
  84.2 5.8 slice-start
  85.2 4.8 slice-start.1
  161.5 5.3 copy-start.21
  166.8 6.2 copy-start
  166.9 6.2 copy-start.18
  166.9 6.2 copy-start.19
  173.0 2.3 copy-start.2
  242.5 5.3 copy-start.22
  320.7 5.3 copy-start.23
  326.0 6.1 copy-start.4
  326.0 6.1 copy-start.17
  332.1 2.3 copy-start.6
  401.6 5.3 copy-start.24
  479.6 5.3 copy-start.25
  479.6 13.5 %copy-start.7 = (f32[2,2,2,128,1024]{4,3,2,0,1:T(8,128)S(1)}, f32[2,2,2,128,1024]{4,3,2,0,1:T(8,128)}, u32[]{:S(2)}) copy-start(f32[2,2,2,128,1024]{4,3,2,0,1:T(8,128)} %copy-done.6) | copy-start | bytes 12582916
  485.0 8.2 %copy-start.9 = (f32[2,2,2,128,1024]{4,3,2,0,1:T(8,128)}, f32[2,2,2,128,1024]{4,3,2,0,1:T(8,128)S(1)}, u32[]{:S(2)}) copy-start(f32[2,2,2,128,1024]{4,3,2,0,1:T(8,128)S(1)} %fusion.24) | copy-start | bytes 12582916
  485.0 8.2 %copy-start.1 = (f32[2,2,2,128,1024]{4,3,2,0,1:T(8,128)S(1)}, f32[2,2,2,128,1024]{4,3,2,0,1:T(8,128)}, u32[]{:S(2)}) copy-start(f32[2,2,2,128,1024]{4,3,2,0,1:T(8,128)} %copy-done) | copy-start | bytes 12582916
  485.0 8.2 %copy-start.3 = (f32[2,2,2,128,1024]{4,3,2,0,1:T(8,128)S(1)}, f32[2,2,2,128,1024]{4,3,2,0,1:T(8,128)}, u32[]{:S(2)}) copy-start(f32[2,2,2,128,1024]{4,3,2,0,1:T(8,128)} %copy-done.2) | copy-start | bytes 12582916
  485.0 8.2 %copy-start.5 = (f32[2,2,2,128,1024]{4,3,2,0,1:T(8,128)S(1)}, f32[2,2,2,128,1024]{4,3,2,0,1:T(8,128)}, u32[]{:S(2)}) copy-start(f32[2,2,2,128,1024]{4,3,2,0,1:T(8,128)} %copy-done.4) | copy-start | bytes 12582916
  499.6 6.2 copy-start.10
  499.6 6.7 copy-start.14
  499.6 6.7 copy-start.15
  505.9 1.6 copy-start.11
  505.9 2.2 copy-start.12
  505.9 2.9 copy-start.13
  505.9 2.8 copy-start.29
  511.3 34.6 %all-gather.9.cloned.1.call-start = ((), (), s32[]{:S(2)}) async-start(), calls=%async_computation.9 | async-start | bytes 1310720 | tf_op jit(solution)/shard_map/all_gather | solution.py:8
  512.1 52.2 %all-gather.11.cloned.1.call-start = ((), (), s32[]{:S(2)}) async-start(), calls=%async_computation.10 | async-start | bytes 1310720 | tf_op jit(solution)/shard_map/all_gather | solution.py:8
  569.5 31.9 %all-to-all-start.7 = ((bf16[3,8,16384]{2,0,1:T(4,128)(2,1)}), bf16[3,8,16384]{2,0,1:T(4,128)(2,1)S(1)}, u32[]{:S(2)}, u32[]{:S(2)}) async-start(bf16[3,8,16384]{2,0,1:T(4,128)(2,1)} %reshape.290), calls=%async_computation.7 | async-start | bytes 2097152 | tf_op jit(solution)/shard_map/all_to_all | solution.py:115
  575.3 1.9 copy-start.16
  601.4 52.1 %all-to-all-start.6 = ((bf16[2,2,2,8,16384]{4,2,1,0,3:T(2,128)(2,1)}), bf16[2,2,2,8,16384]{4,2,1,0,3:T(2,128)(2,1)S(1)}, u32[]{:S(2)}, u32[]{:S(2)}) async-start(bf16[2,2,2,8,16384]{4,2,1,0,3:T(2,128)(2,1)} %copy.317), calls=%async_computation.6 | async-start | bytes 4194304 | tf_op jit(solution)/shard_map/all_to_all | solution.py:105
Sparse Core Ops, SparseCore 0:
  511.5 15.6 all-gather.6
  529.3 16.6 all-gather.8
  547.5 16.6 all-gather.10
